TPU v7x, 32 devices: a whole 2x2x4 slice. The times are simulated.
32 devices in a mesh: dir: 2 (over y), row: 4 (over z), col: 4 (over x, core).
Axes of the slice: x: 2, y: 2, z: 4, core: 2. Of those that a mesh axis runs over, the one named last changes fastest.
Arguments:
- cotangent: bfloat16 [2048, 512], P('dir'), may hold values from -3 to 3
- radiation: bfloat16 [2, 8192, 2048], P(None, ('row', 'col'), 'dir'), may hold values from -0.125 to 0.125
- near_z: float32 [2, 256, 512, 512], P(None, ('dir', 'row', 'col')), may hold values from -0.25 to 0.25
- near_pairs: int32 [256, 2], P(('dir', 'row', 'col')), may hold values from 0 to 15, as said below
- far_ut: float32 [2, 128, 96, 512], P(None, ('dir', 'row', 'col')), may hold values from -0.25 to 0.25
- far_vt: float32 [2, 128, 96, 512], P(None, ('dir', 'row', 'col')), may hold values from -0.625 to 0.625
- far_pairs: int32 [128, 2], P(('dir', 'row', 'col')), may hold values from 0 to 15, as said below
- far_ranks: int32 [128], P(('dir', 'row', 'col')), may hold values from 32 to 96
- block_counts: int32 [32, 2], P(('dir', 'row', 'col')), may hold values from 1 to 8, as said below
Outputs:
- adjoint: float32 [8192, 512], P(('col', 'dir', 'row'))
Inputs may be any that keep to these rules, and one draw needn't show every extreme that they name: `near_pairs`: slot s belongs to the device at position g = s div 8 in the order dir, row, col, with row index r and column index c; its row cluster lies in r * 4 to (r + 1) * 4 - 1 and its column cluster in c * 4 to (c + 1) * 4 - 1. Pairs may repeat. `far_pairs`: slot s belongs to the device at position s div 4 in the order dir, row, col, with row index r and column index c; its row cluster lies in r * 4 to (r + 1) * 4 - 1 and its column cluster in c * 4 to (c + 1) * 4 - 1. Pairs may repeat. `block_counts`: column 0 is at most 8 and column 1 at most 4; the live slots of a device are its first ones.
All inputs are finite; a program needn't handle non-finite values.
Results may differ from a plain program's by a relative error of at most 0.0003.
Values sent between devices are 32-bit elements; how exact they have to be, the bound alone decides.
A program may use at most 128 MiB of HBM per device.

v0:
```python
import functools

import jax
import jax.numpy as jnp
from jax import lax
from jax.experimental import pallas as pl
from jax.experimental.pallas import tpu as pltpu
from jax.sharding import PartitionSpec as P

CHUNKS = 4
CORES = 2
MESH = pl.DeviceIdType.MESH
F32 = jnp.float32
BF16 = jnp.bfloat16
NT = (((1,), (1,)), ((), ()))


def dot(left, right):
    return jnp.dot(left, right, preferred_element_type=F32)


def dot_nt(left, right):
    return lax.dot_general(left, right, NT, preferred_element_type=F32)


def split(values):
    high = values.astype(BF16)
    return high, (values - high.astype(F32)).astype(BF16)


def swap_rows(values):
    half = values.shape[0] // 2
    return jnp.concatenate([-values[half:], values[:half]], axis=0)


def fold(values):
    half = values.shape[0] // 2
    return values[:half] + values[half:]


def kernel(
    n_dir, n_row, n_col, depth,
    near_pairs, far_pairs, far_ranks, counts, cot, rad, near_z, far_ut, far_vt,
    out,
    z_high, z_low, stage, far_stage, left_far, right_far, cot_t, totals, sent, dir_in, gathered, sides, terms, parts, dir_parts, sums, row_parts,
    stage_sem, far_sem, d_send, d_recv, x_send, x_recv, c_send, c_recv, p_send, p_recv, r_send, r_recv,
):
    chunks, width = sent.shape[0], sent.shape[1]
    half = width // 2
    wide = cot.shape[1]
    stages = stage.shape[0]
    rank_most, rank_pad = far_ut.shape[2], left_far.shape[2] // 2
    n_near, n_far = near_z.shape[1], far_ut.shape[1]
    block = near_z.shape[2]
    piece = block // n_dir
    n_x = n_col // CORES
    per_dir = n_row // n_dir
    d = lax.axis_index("dir")
    r = lax.axis_index("row")
    c = lax.axis_index("col")
    x, core = c // CORES, c % CORES
    partner = x * CORES + (CORES - 1 - core)

    def dir_peer(j):
        return (lax.rem(d + j, n_dir), r, c)

    def x_peer(j):
        return (d, r, lax.rem(x + j, n_x) * CORES + core)

    def row_peer(i):
        return (d, lax.rem(r + i, n_row), c)

    def from_x(j, core_of):
        return lax.rem(x + n_x - j, n_x) * CORES + core_of

    def remote(src, dst, send, recv, device):
        return pltpu.make_async_remote_copy(
            src_ref=src, dst_ref=dst, send_sem=send, recv_sem=recv, device_id=device, device_id_type=MESH
        )

    def load_item(item):
        slot, part = item // 2, lax.rem(item, 2)
        return pltpu.make_async_copy(
            near_z.at[part, slot], stage.at[lax.rem(item, stages)], stage_sem.at[lax.rem(item, stages)]
        )

    for item in range(stages):
        load_item(item).start()
    def load_far(s):
        side = lax.rem(s, 2)
        return [
            pltpu.make_async_copy(source.at[part, s], far_stage.at[side, 2 * i + part], far_sem.at[side, 2 * i + part])
            for i, source in enumerate((far_ut, far_vt))
            for part in range(2)
        ]

    for s in range(min(2, n_far)):
        for load in load_far(s):
            load.start()

    peers = [dir_peer(j) for j in range(1, n_dir)]
    peers += [x_peer(j) for j in range(1, n_x)]
    peers += [row_peer(i) for i in range(1, n_row)]
    peers.append((d, r, partner))
    barrier = pltpu.get_barrier_semaphore()
    for device in peers:
        pl.semaphore_signal(barrier, inc=1, device_id=device, device_id_type=MESH)
    pl.semaphore_wait(barrier, len(peers))

    def send_dir(k, j):
        return remote(sent.at[k], dir_in.at[k, j - 1], d_send.at[k, j - 1], d_recv.at[k, j - 1], dir_peer(j))

    def send_x(k, j):
        return remote(gathered.at[k, c], gathered.at[k, c], x_send.at[k, j - 1], x_recv.at[k, j - 1], x_peer(j))

    def send_core(k, j, core_of):
        which = from_x(j, core_of)
        return remote(
            gathered.at[k, which], gathered.at[k, which], c_send.at[k, j], c_recv.at[k, j], (d, r, partner)
        )

    def send_part(k, j, q):
        owner = lax.rem(d + j, n_dir)
        return remote(
            parts.at[k % depth, owner * n_row + q],
            dir_parts.at[k, j - 1, q],
            p_send.at[k, j - 1, q],
            p_recv.at[k, j - 1, q],
            dir_peer(j),
        )

    def send_row(k, q):
        return remote(
            sums.at[k, q], row_parts.at[k, r], r_send.at[k, q], r_recv.at[k, r], (d, q, c)
        )

    def right_sides(k):
        left = jnp.concatenate(
            [cot_t[k * half : (k + 1) * half], cot_t[wide // 2 + k * half : wide // 2 + (k + 1) * half]], axis=0
        )
        sent[k] = dot_nt(left, rad[0]) + dot_nt(swap_rows(left), rad[1])
        for j in range(1, n_dir):
            send_dir(k, j).start()

    def convert(first, last):
        def body(item, carry):
            load_item(item).wait()
            high, low = split(stage[lax.rem(item, stages)])
            rows = pl.ds(pl.multiple_of(lax.rem(item, 2) * block, block), block)
            z_high[item // 2, rows, :] = high
            z_low[item // 2, rows, :] = low

            @pl.when(item + stages < 2 * n_near)
            def _():
                load_item(item + stages).start()

            return carry

        lax.fori_loop(2 * first, 2 * last, body, 0)

    def pack_far():
        rest = jnp.zeros((rank_pad - rank_most, block), F32)

        def body(s, carry):
            for load in load_far(s):
                load.wait()
            side = lax.rem(s, 2)
            for part in range(2):
                factor = jnp.concatenate([far_stage[side, part], rest], axis=0)
                high, low = split(factor.T)
                rows = slice(part * block, (part + 1) * block)
                left_far[s, rows, :rank_pad] = high
                left_far[s, rows, rank_pad:] = low
                factor = jnp.concatenate([far_stage[side, 2 + part], rest], axis=0)
                high, low = split(factor)
                rows = slice(part * rank_pad, (part + 1) * rank_pad)
                right_far[0, s, rows, :] = high
                right_far[1, s, rows, :] = low

            @pl.when(s + 2 < n_far)
            def _():
                for load in load_far(s + 2):
                    load.start()

            return carry

        lax.fori_loop(0, n_far, body, 0)

    def add_dirs(k):
        for j in range(1, n_dir):
            send_dir(k, j).wait_recv()
        total = sent[k]
        for j in range(1, n_dir):
            total = total + dir_in[k, j - 1]
        gathered[k, c] = total
        for j in range(1, n_x):
            send_x(k, j).start()
        send_core(k, 0, core).start()

    def relay(k):
        for j in range(1, n_x):
            which = from_x(j, core)
            remote(
                gathered.at[k, which], gathered.at[k, which], x_send.at[k, j - 1], x_recv.at[k, j - 1], x_peer(j)
            ).wait_recv()
            send_core(k, j, core).start()

    def products(k):
        for j in range(n_x):
            send_core(k, j, CORES - 1 - core).wait_recv()

        def side(q, carry):
            values = gathered[k, q]
            high, low = split(jnp.concatenate([values, swap_rows(values)], axis=1))
            sides[q, :width] = high
            sides[q, width:] = low
            return carry

        lax.fori_loop(0, n_col, side, 0)

        per_far = n_near // n_far

        def near(s):
            left = sides[lax.rem(near_pairs[s, 0], n_col)]
            terms[s] = fold(dot(left, z_high[s])) + dot(left[:width], z_low[s])

        def body(s, carry):
            both = dot(sides[lax.rem(far_pairs[s, 0], n_col)], left_far[s])
            near(s * per_far)
            coeffs = fold(both[:, :rank_pad]) + both[:width, rank_pad:]
            lanes = lax.broadcasted_iota(jnp.int32, coeffs.shape, 1)
            coeffs = jnp.where(lanes < far_ranks[s], coeffs, 0.0)
            high, low = split(jnp.concatenate([coeffs, swap_rows(coeffs)], axis=1))
            for i in range(1, per_far):
                near(s * per_far + i)
            both = dot(jnp.concatenate([high, low], axis=0), right_far[0, s])
            terms[n_near + s] = fold(both) + dot(high, right_far[1, s])
            return carry

        lax.fori_loop(0, n_far, body, 0)

        if k >= depth:
            for j in range(1, n_dir):
                for q in range(n_row):
                    send_part(k - depth, j, q).wait_send()
        for t in range(n_row):
            j, q0 = 1 + t // per_dir, (t % per_dir) * n_dir
            cluster = lax.rem(lax.rem(d + j, n_dir) * per_dir + t % per_dir, n_row)
            target = c * n_row + cluster
            gains = [
                jnp.where((near_pairs[s, 1] == target) & (s < counts[0, 0]), 1.0, 0.0) for s in range(n_near)
            ] + [
                jnp.where((far_pairs[s, 1] == target) & (s < counts[0, 1]), 1.0, 0.0) for s in range(n_far)
            ]
            for h in range(n_dir):
                lanes = slice(h * piece, (h + 1) * piece)
                total = terms[0, :, lanes] * gains[0]
                for s in range(1, n_near + n_far):
                    total = total + terms[s, :, lanes] * gains[s]
                parts[k % depth, cluster * n_dir + h] = total
                if j < n_dir:
                    send_part(k, j, q0 + h).start()
        for q in range(n_row):
            sums[k, q] = parts[k % depth, d * n_row + q]

    def add_parts(k):
        for q in range(n_row):
            for j in range(1, n_dir):
                send_part(k, j, q).wait_recv()
                sums[k, q] = sums[k, q] + dir_parts[k, j - 1, q]

            @pl.when(q != r)
            def _():
                send_row(k, q).start()

    def finish(k):
        total = sums[k, r]
        for i in range(1, n_row):
            src = lax.rem(r + i, n_row)
            remote(
                sums.at[k, src], row_parts.at[k, src], r_send.at[k, src], r_recv.at[k, src], row_peer(i)
            ).wait_recv()
            total = total + row_parts[k, src]
        totals[k * half : (k + 1) * half] = total[:half]
        totals[wide // 2 + k * half : wide // 2 + (k + 1) * half] = total[half:]
        if k % group == group - 1:
            for base in (0, wide // 2):
                columns = slice(base + (k + 1 - group) * half, base + (k + 1) * half)
                out[:, columns] = totals[columns].T

    group = max(1, 128 // half)
    cot_t[...] = cot[...].T
    for k in range(chunks):
        right_sides(k)
    steps = chunks
    edges = [n_near * i // steps for i in range(steps + 1)]
    for i in range(steps):
        convert(edges[i], edges[i + 1])
        if i < chunks - 1:
            add_dirs(i)
        if i >= 1:
            relay(i - 1)
    pack_far()
    products(0)
    add_dirs(chunks - 1)
    for k in range(1, chunks):
        products(k) if k < chunks - 1 else None
        if k == 1:
            relay(chunks - 1)
        if k == chunks - 1:
            add_parts(0)
            products(k)
    for k in range(1, chunks):
        add_parts(k)
        finish(k - 1)
    finish(chunks - 1)

    for k in range(chunks):
        for j in range(1, n_dir):
            send_dir(k, j).wait_send()
            if k >= chunks - depth:
                for q in range(n_row):
                    send_part(k, j, q).wait_send()
        for j in range(1, n_x):
            send_x(k, j).wait_send()
        for j in range(n_x):
            send_core(k, j, core).wait_send()
        for q in range(n_row):

            @pl.when(q != r)
            def _():
                send_row(k, q).wait_send()


def shards(
    cotangent, radiation, near_z, near_pairs, far_ut, far_vt, far_pairs, far_ranks, block_counts
):
    n_dir, n_row, n_col = (lax.axis_size(name) for name in ("dir", "row", "col"))
    deep, wide = cotangent.shape
    chunks, width = CHUNKS, wide // CHUNKS
    block = near_z.shape[2]
    n_near, n_far, rank_most = near_z.shape[1], far_ut.shape[1], far_ut.shape[2]
    n_x = n_col // CORES
    piece = block // n_dir
    small = n_row * n_col <= 16
    depth = chunks if small else 2
    stages = min(6 if small else 2, 2 * n_near)
    rank_pad = -(-rank_most // 128) * 128
    vmem = pl.BlockSpec(memory_space=pltpu.VMEM)
    smem = pl.BlockSpec(memory_space=pltpu.SMEM)
    anywhere = pl.BlockSpec(memory_space=pl.ANY)
    dma = pltpu.SemaphoreType.DMA
    return pl.pallas_call(
        functools.partial(kernel, n_dir, n_row, n_col, depth),
        out_shape=jax.ShapeDtypeStruct((piece, wide), F32),
        in_specs=[smem] * 4 + [vmem] * 2 + [anywhere] * 3,
        out_specs=vmem,
        scratch_shapes=[
            pltpu.VMEM((n_near, 2 * block, block), BF16),
            pltpu.VMEM((n_near, 2 * block, block), BF16),
            pltpu.VMEM((stages, block, block), F32),
            pltpu.VMEM((2, 4, rank_most, block), F32),
            pltpu.VMEM((n_far, 2 * block, 2 * rank_pad), BF16),
            pltpu.VMEM((2, n_far, 2 * rank_pad, block), BF16),
            pltpu.VMEM((wide, deep), BF16),
            pltpu.VMEM((wide, piece), F32),
            pltpu.VMEM((chunks, width, block), F32),
            pltpu.VMEM((chunks, n_dir - 1, width, block), F32),
            pltpu.VMEM((chunks, n_col, width, block), F32),
            pltpu.VMEM((n_col, 2 * width, 2 * block), BF16),
            pltpu.VMEM((n_near + n_far, width, block), F32),
            pltpu.VMEM((depth, n_dir * n_row, width, piece), F32),
            pltpu.VMEM((chunks, n_dir - 1, n_row, width, piece), F32),
            pltpu.VMEM((chunks, n_row, width, piece), F32),
            pltpu.VMEM((chunks, n_row, width, piece), F32),
            dma((stages,)),
            dma((2, 4)),
            dma((chunks, n_dir - 1)),
            dma((chunks, n_dir - 1)),
            dma((chunks, n_x - 1)),
            dma((chunks, n_x - 1)),
            dma((chunks, n_x)),
            dma((chunks, n_x)),
            dma((chunks, n_dir - 1, n_row)),
            dma((chunks, n_dir - 1, n_row)),
            dma((chunks, n_row)),
            dma((chunks, n_row)),
        ],
        compiler_params=pltpu.CompilerParams(
            collective_id=0, has_side_effects=True, vmem_limit_bytes=67043328
        ),
    )(near_pairs, far_pairs, far_ranks, block_counts, cotangent, radiation, near_z, far_ut, far_vt)


def solution(mesh):
    return jax.shard_map(
        shards,
        mesh=mesh,
        in_specs=(
            P("dir", None),
            P(None, ("row", "col"), "dir"),
            P(None, ("dir", "row", "col"), None, None),
            P(("dir", "row", "col"), None),
            P(None, ("dir", "row", "col"), None, None),
            P(None, ("dir", "row", "col"), None, None),
            P(("dir", "row", "col"), None),
            P(("dir", "row", "col")),
            P(("dir", "row", "col"), None),
        ),
        out_specs=P(("col", "dir", "row"), None),
        check_vma=False,
    )
```

profile of v0, /device:TPU:0, one launch (start us, length us, event | category | flops | bytes accessed | tf_op | source)
XLA Modules:
  0.0 103.7 jit_solution(14015752977729101451)
XLA Ops:
  0.0 1.4 %copy.11.far_pairs = s32[4,2]{1,0:T(4,128)} copy(s32[4,2]{0,1:T(2,128)} %param.15) | data formatting | bytes 64 | tf_op args[6]
  1.4 1.3 %copy.10.near_pairs = s32[8,2]{1,0:T(8,128)} copy(s32[8,2]{0,1:T(2,128)} %param.12) | data formatting | bytes 128 | tf_op args[3]
  2.7 99.1 %shard_map.91 = f32[256,512]{1,0:T(8,128)} custom-call(s32[8,2]{1,0:T(8,128)} %copy.10.near_pairs, s32[4,2]{1,0:T(4,128)} %copy.11.far_pairs, s32[4]{0:T(128)} %far_ranks.1, s32[1,2]{1,0:T(1,128)} %counts.1, bf16[1024,512]{1,0:T(8,128)(2,1)} %cot.1, bf16[2,512,1024]{2,1,0:T(8,128)(2,1)} %rad.1, f32[2,8,512,512]{3,2,1,0:T(8,128)} %near_z.1, ...), custom_call_target="tpu_custom_call" | custom-call | tf_op jit(solution)/shard_map/pallas_call | solution.py:353
  101.8 1.9 %copy.13 = f32[256,512]{1,0:T(8,128)} copy(f32[256,512]{1,0:T(8,128)} %shard_map.91) | data formatting | bytes 1048576
where the time goes:
time: 104 us
  Pallas kernels  99.1 us (95%)
  local copies, waits for them, and re-layouts  4.56 us (4%)
    pallas_call x1, Pallas kernels, shards(): pl.pallas_call(functools.partial(kernel, n_dir, n_row, n_col, depth), out...  99.1 us
    unnamed x3, local copies, waits for them, and re-layouts  4.56 us

commit v1 on v0

v1 whole, which is shorter than its diff:
```python
import functools

import jax
import jax.numpy as jnp
from jax import lax
from jax.experimental import pallas as pl
from jax.experimental.pallas import tpu as pltpu
from jax.sharding import PartitionSpec as P

CORES = 2
MESH = pl.DeviceIdType.MESH
F32 = jnp.float32
BF16 = jnp.bfloat16
NT = (((1,), (1,)), ((), ()))
PARTS = 8
SIZES = (1, 1, 2, 2, 2)
ROW_FIRST = (1.0, 0.0, 0.5, 0.0, 0.0)


def dot(left, right):
    return jnp.dot(left, right, preferred_element_type=F32)


def dot_nt(left, right):
    return lax.dot_general(left, right, NT, preferred_element_type=F32)


def split(values):
    high = values.astype(BF16)
    return high, (values - high.astype(F32)).astype(BF16)


def swap_rows(values):
    half = values.shape[0] // 2
    return jnp.concatenate([-values[half:], values[:half]], axis=0)


def fold(values):
    half = values.shape[0] // 2
    return values[:half] + values[half:]


class Plan:
    def __init__(self, wide, n_row):
        unit = wide // 2 // PARTS
        self.half = [unit * size for size in SIZES]
        self.width = [2 * half for half in self.half]
        self.first = [sum(self.half[:k]) for k in range(len(self.half))]
        self.row_wide = [int(width * share) for width, share in zip(self.width, ROW_FIRST)]
        self.row_at = [sum(self.row_wide[:k]) for k in range(len(self.half))]
        self.row_total = max(8, sum(self.row_wide))
        self.chunks = len(self.half)
        self.offsets = sorted(range(1, n_row), key=lambda o: -min(o, n_row - o)) + [0]

    def rows(self, k):
        return slice(2 * self.first[k], 2 * self.first[k] + self.width[k])

    def dir_rows(self, k):
        start = 2 * self.first[k]
        return slice(start, start + self.width[k] - self.row_wide[k])

    def row_rows(self, k):
        stop = 2 * self.first[k] + self.width[k]
        return slice(stop - self.row_wide[k], stop)

    def row_slots(self, k):
        return slice(self.row_at[k], self.row_at[k] + self.row_wide[k])


def kernel(
    n_dir, n_row, n_col, plan,
    near_pairs, far_pairs, far_ranks, counts, cot_hbm, rad_hbm, near_z, far_ut, far_vt,
    out,
    placed, cot, rad, z_high, z_low, stage, far_stage, left_far, right_far, cot_t, totals, sent, dir_in, gathered, sides, terms,
    parts, dir_parts, row_parts, pair_in, row_in, last_in,
    in_sem, stage_sem, far_sem, d_send, d_recv, x_send, x_recv, c_send, c_recv, p_send, p_recv, r_send, r_recv,
    a_recv, q_send, q_recv, l_send, l_recv, o_sem,
):
    chunks = plan.chunks
    wide = cot.shape[1]
    stages = stage.shape[0]
    rank_most, rank_pad = far_ut.shape[2], left_far.shape[2] // 2
    n_near, n_far = near_z.shape[1], far_ut.shape[1]
    block = near_z.shape[2]
    piece = block // n_dir
    n_x = n_col // CORES
    per_dir = n_row // n_dir
    n_off = len(plan.offsets)
    d = lax.axis_index("dir")
    r = lax.axis_index("row")
    c = lax.axis_index("col")
    x, core = c // CORES, c % CORES
    partner = x * CORES + (CORES - 1 - core)
    row_pair = r + 1 - 2 * lax.rem(r, 2)

    def dir_peer(j):
        return (lax.rem(d + j, n_dir), r, c)

    def x_peer(j):
        return (d, r, lax.rem(x + j, n_x) * CORES + core)

    def row_peer(i):
        return (d, lax.rem(r + plan.offsets[i], n_row), c)

    def from_x(j, core_of):
        return lax.rem(x + n_x - j, n_x) * CORES + core_of

    def remote(src, dst, send, recv, device):
        return pltpu.make_async_remote_copy(
            src_ref=src, dst_ref=dst, send_sem=send, recv_sem=recv, device_id=device, device_id_type=MESH
        )

    peers = [dir_peer(j) for j in range(1, n_dir)]
    peers += [x_peer(j) for j in range(1, n_x)]
    peers += [row_peer(i) for i in range(n_off - 1)]
    peers.append((d, r, partner))
    barrier = pltpu.get_barrier_semaphore()
    for device in peers:
        pl.semaphore_signal(barrier, inc=1, device_id=device, device_id_type=MESH)

    inputs = [pltpu.make_async_copy(cot_hbm, cot, in_sem.at[0])]
    inputs += [pltpu.make_async_copy(rad_hbm.at[part], rad.at[part], in_sem.at[1 + part]) for part in range(2)]
    for load in inputs:
        load.start()

    def load_item(item):
        slot, part = item // 2, lax.rem(item, 2)
        return pltpu.make_async_copy(
            near_z.at[part, slot], stage.at[lax.rem(item, stages)], stage_sem.at[lax.rem(item, stages)]
        )

    def load_far(s):
        side = lax.rem(s, 2)
        return [
            pltpu.make_async_copy(source.at[part, s], far_stage.at[side, 2 * i + part], far_sem.at[side, 2 * i + part])
            for i, source in enumerate((far_ut, far_vt))
            for part in range(2)
        ]

    def send_dir(k, j):
        rows = plan.rows(k)
        return remote(sent.at[rows], dir_in.at[j - 1, rows], d_send.at[k, j - 1], d_recv.at[k, j - 1], dir_peer(j))

    def send_x(k, j, which=None):
        block_of = gathered.at[c if which is None else which, plan.rows(k)]
        return remote(block_of, block_of, x_send.at[k, j - 1], x_recv.at[k, j - 1], x_peer(j))

    def send_core(k, j, core_of):
        block_of = gathered.at[from_x(j, core_of), plan.rows(k)]
        return remote(block_of, block_of, c_send.at[k, j], c_recv.at[k, j], (d, r, partner))

    def send_part(k, j, i):
        rows = plan.dir_rows(k)
        return remote(
            parts.at[j, i, rows], dir_parts.at[j - 1, i, rows], p_send.at[k, j - 1, i], p_recv.at[k, j - 1, i], dir_peer(j)
        )

    def send_row(k, i):
        rows = plan.dir_rows(k)
        return remote(parts.at[0, i, rows], row_parts.at[i, rows], r_send.at[k, i], r_recv.at[k, i], row_peer(i))

    def row_of(i):
        return lax.rem(r + plan.offsets[i], n_row)

    def same_pair(i):
        return row_of(i) // 2 == r // 2

    def gathers(i):
        above = row_of(i) > r
        odd = lax.rem(r, 2) == 1
        return jnp.logical_not(same_pair(i)) & (above == odd)

    def send_pair(k, i, j):
        return remote(
            parts.at[j, i, plan.row_rows(k)],
            pair_in.at[row_of(i), j, plan.row_slots(k)],
            q_send.at[k, i, j],
            a_recv.at[k, row_of(i), j],
            (d, row_pair, c),
        )

    def send_sum(k, i, j):
        return remote(
            parts.at[j, i, plan.row_rows(k)],
            row_in.at[r // 2, j, plan.row_slots(k)],
            q_send.at[k, i, j],
            q_recv.at[k, r // 2, j],
            row_peer(i),
        )

    def send_last(k, j):
        return remote(
            parts.at[j, n_off - 1, plan.row_rows(k)],
            last_in.at[j - 1, plan.row_slots(k)],
            l_send.at[k, j - 1],
            l_recv.at[k, j - 1],
            dir_peer(j),
        )

    def right_sides(k):
        at, half = plan.first[k], plan.half[k]
        left = jnp.concatenate([cot_t[at : at + half], cot_t[wide // 2 + at : wide // 2 + at + half]], axis=0)
        sent[plan.rows(k)] = dot_nt(left, rad[0]) + dot_nt(swap_rows(left), rad[1])

    def convert(first, last):
        def body(item, carry):
            load_item(item).wait()
            high, low = split(stage[lax.rem(item, stages)])
            rows = pl.ds(pl.multiple_of(lax.rem(item, 2) * block, block), block)
            z_high[item // 2, rows, :] = high
            z_low[item // 2, rows, :] = low

            @pl.when(item + stages < 2 * n_near)
            def _():
                load_item(item + stages).start()

            return carry

        lax.fori_loop(2 * first, 2 * last, body, 0)

    def pack_far():
        rest = jnp.zeros((rank_pad - rank_most, block), F32)

        def body(s, carry):
            for load in load_far(s):
                load.wait()
            side = lax.rem(s, 2)
            for part in range(2):
                factor = jnp.concatenate([far_stage[side, part], rest], axis=0)
                high, low = split(factor.T)
                rows = slice(part * block, (part + 1) * block)
                left_far[s, rows, :rank_pad] = high
                left_far[s, rows, rank_pad:] = low
                factor = jnp.concatenate([far_stage[side, 2 + part], rest], axis=0)
                high, low = split(factor)
                rows = slice(part * rank_pad, (part + 1) * rank_pad)
                right_far[0, s, rows, :] = high
                right_far[1, s, rows, :] = low

            @pl.when(s + 2 < n_far)
            def _():
                for load in load_far(s + 2):
                    load.start()

            return carry

        lax.fori_loop(0, n_far, body, 0)

    def add_dirs(k):
        rows = plan.rows(k)
        for j in range(1, n_dir):
            send_dir(k, j).wait_recv()
        total = sent[rows]
        for j in range(1, n_dir):
            total = total + dir_in[j - 1, rows]
        gathered[c, rows] = total
        for j in range(1, n_x):
            send_x(k, j).start()
        send_core(k, 0, core).start()

    def relay(k):
        for j in range(1, n_x):
            send_x(k, j, from_x(j, core)).wait_recv()
            send_core(k, j, core).start()

    def products(k, between=None):
        between = {min(stop, n_far): calls for stop, calls in (between or {}).items()}
        width, rows = plan.width[k], plan.rows(k)
        for j in range(n_x):
            send_core(k, j, CORES - 1 - core).wait_recv()

        def side(q, carry):
            values = gathered[q, rows]
            high, low = split(jnp.concatenate([values, swap_rows(values)], axis=1))
            sides[q, :width] = high
            sides[q, width : 2 * width] = low
            return carry

        lax.fori_loop(0, n_col, side, 0)

        per_far = n_near // n_far

        def near(s):
            left = sides[lax.rem(near_pairs[0, s], n_col), : 2 * width]
            terms[s, :width] = fold(dot(left, z_high[s])) + dot(left[:width], z_low[s])

        def body(s, carry):
            both = dot(sides[lax.rem(far_pairs[0, s], n_col), : 2 * width], left_far[s])
            near(s * per_far)
            coeffs = fold(both[:, :rank_pad]) + both[:width, rank_pad:]
            lanes = lax.broadcasted_iota(jnp.int32, coeffs.shape, 1)
            coeffs = jnp.where(lanes < far_ranks[s], coeffs, 0.0)
            high, low = split(jnp.concatenate([coeffs, swap_rows(coeffs)], axis=1))
            for i in range(1, per_far):
                near(s * per_far + i)
            both = dot(jnp.concatenate([high, low], axis=0), right_far[0, s])
            terms[n_near + s, :width] = fold(both) + dot(high, right_far[1, s])
            return carry

        at = 0
        for stop in sorted({*between, n_far}):
            if stop > at:
                lax.fori_loop(at, stop, body, 0)
            at = stop
            for call, i in between.pop(stop, ()):
                call(i)

        for j in list(range(1, n_dir)) + [0]:
            for i in range(n_off):
                q = row_of(i)
                target = c * n_row + lax.rem(d + j, n_dir) * per_dir + q // n_dir
                lanes = pl.ds(pl.multiple_of(lax.rem(q, n_dir) * piece, piece), piece)
                gains = [
                    jnp.where((near_pairs[1, s] == target) & (s < counts[0, 0]), 1.0, 0.0) for s in range(n_near)
                ] + [jnp.where((far_pairs[1, s] == target) & (s < counts[0, 1]), 1.0, 0.0) for s in range(n_far)]
                total = terms[0, :width, lanes] * gains[0]
                for s in range(1, n_near + n_far):
                    total = total + terms[s, :width, lanes] * gains[s]
                parts[j, i, rows] = total
                if j > 0 and plan.row_wide[k] < width:
                    send_part(k, j, i).start()
                if i < n_off - 1 and plan.row_wide[k] > 0:
                    own = same_pair(i)
                    mine = gathers(i)

                    @pl.when(own)
                    def _():
                        send_sum(k, i, j).start()

                    @pl.when(jnp.logical_not(own | mine))
                    def _():
                        send_pair(k, i, j).start()

    def add_parts(k, first=0, last=n_off):
        if plan.row_wide[k] == plan.width[k]:
            return
        rows = plan.dir_rows(k)
        for i in range(first, last):
            total = parts[0, i, rows]
            for j in range(1, n_dir):
                send_part(k, j, i).wait_recv()
                total = total + dir_parts[j - 1, i, rows]
            parts[0, i, rows] = total
            if i < n_off - 1:
                send_row(k, i).start()

    def add_pairs(k):
        if plan.row_wide[k] == 0:
            return
        rows, slots = plan.row_rows(k), plan.row_slots(k)
        for j in list(range(1, n_dir)) + [0]:
            for i in range(n_off - 1):

                @pl.when(gathers(i))
                def _():
                    send_pair(k, i, j).wait_recv()
                    parts[j, i, rows] = parts[j, i, rows] + pair_in[row_of(i), j, slots]
                    send_sum(k, i, j).start()

    def add_rows(k):
        if plan.row_wide[k] == 0:
            return
        rows, slots = plan.row_rows(k), plan.row_slots(k)
        for j in list(range(1, n_dir)) + [0]:
            total = parts[j, n_off - 1, rows]
            for p in range(n_row // 2):
                remote(
                    parts.at[j, n_off - 1, rows], row_in.at[p, j, slots], l_send.at[k, 0], q_recv.at[k, p, j], row_peer(0)
                ).wait_recv()
                total = total + row_in[p, j, slots]
            parts[j, n_off - 1, rows] = total
            if j > 0:
                send_last(k, j).start()

    def place(k, start, total):
        half, at = plan.half[k], plan.first[k]
        stop = start + total.shape[0]
        if start < half:
            cut = min(stop, half)
            totals[at + start : at + cut] = total[: cut - start]
        if stop > half:
            cut = max(start, half)
            base = wide // 2 + at - half
            totals[base + cut : base + stop] = total[cut - start :]

    def finish_dir(k):
        if plan.row_wide[k] == plan.width[k]:
            return
        rows = plan.dir_rows(k)
        total = parts[0, n_off - 1, rows]
        for i in range(n_off - 1):
            send_row(k, i).wait_recv()
            total = total + row_parts[i, rows]
        place(k, 0, total)

    def finish_row(k):
        if plan.row_wide[k] == 0:
            return
        rows, slots = plan.row_rows(k), plan.row_slots(k)
        total = parts[0, n_off - 1, rows]
        for j in range(1, n_dir):
            send_last(k, j).wait_recv()
            total = total + last_in[j - 1, slots]
        place(k, plan.width[k] - plan.row_wide[k], total)

    def put(first, last):
        for base in (0, wide // 2):
            columns = slice(base + first, base + last)
            placed[:, columns] = totals[columns].T
            copy = pltpu.make_async_copy(placed.at[:, columns], out.at[:, columns], o_sem.at[len(put_copies)])
            copy.start()
            put_copies.append(copy)

    def drain():
        for k in range(chunks):
            for j in range(1, n_dir):
                send_dir(k, j).wait_send()
            for j in range(1, n_x):
                send_x(k, j).wait_send()
            for j in range(n_x):
                send_core(k, j, core).wait_send()
            if plan.row_wide[k] < plan.width[k]:
                for i in range(n_off):
                    for j in range(1, n_dir):
                        send_part(k, j, i).wait_send()
                    if i < n_off - 1:
                        send_row(k, i).wait_send()
            if plan.row_wide[k] > 0:
                for j in range(n_dir):
                    for i in range(n_off - 1):
                        send_sum(k, i, j).wait_send()
                    if j > 0:
                        send_last(k, j).wait_send()
        for copy in put_copies:
            copy.wait()

    put_copies = []

    for load in inputs:
        load.wait()
    for item in range(stages):
        load_item(item).start()
    for s in range(min(2, n_far)):
        for load in load_far(s):
            load.start()
    cot_t[...] = cot[...].T
    for k in range(chunks):
        right_sides(k)
        if k == 1:
            pl.semaphore_wait(barrier, len(peers))
        for i in ((0, 1) if k == 1 else (k,) if k > 1 else ()):
            for j in range(1, n_dir):
                send_dir(i, j).start()

    convert(0, n_near)
    add_dirs(0)
    pack_far()
    add_dirs(1)
    relay(0)
    products(0, {2: [(relay, 1), (add_dirs, 2)]})
    products(1, {2: [(add_dirs, 3)], 4: [(relay, 2)]})
    products(2, {1: [(add_pairs, 0)], 2: [(add_dirs, 4)], 4: [(relay, 3)]})
    products(3, {1: [(add_rows, 0)], 2: [(add_parts, 1)], 4: [(relay, 4)]})
    products(4, {1: [(add_pairs, 2)], 3: [(add_parts, 2)]})
    add_rows(2)
    finish_row(0)
    finish_dir(1)
    add_parts(3)
    finish_dir(2)
    add_parts(4)
    finish_row(2)
    put(0, plan.first[3])
    finish_dir(3)
    finish_dir(4)
    put(plan.first[3], wide // 2)
    drain()


def shards(
    cotangent, radiation, near_z, near_pairs, far_ut, far_vt, far_pairs, far_ranks, block_counts
):
    n_dir, n_row, n_col = (lax.axis_size(name) for name in ("dir", "row", "col"))
    deep, wide = cotangent.shape
    plan = Plan(wide, n_row)
    chunks, most = plan.chunks, max(plan.width)
    block = near_z.shape[2]
    n_near, n_far, rank_most = near_z.shape[1], far_ut.shape[1], far_ut.shape[2]
    n_x = n_col // CORES
    piece = block // n_dir
    small = n_row * n_col <= 16
    stages = min(6 if small else 2, 2 * n_near)
    rank_pad = -(-rank_most // 128) * 128
    smem = pl.BlockSpec(memory_space=pltpu.SMEM)
    anywhere = pl.BlockSpec(memory_space=pl.ANY)
    dma = pltpu.SemaphoreType.DMA
    return pl.pallas_call(
        functools.partial(kernel, n_dir, n_row, n_col, plan),
        out_shape=jax.ShapeDtypeStruct((piece, wide), F32),
        in_specs=[smem] * 4 + [anywhere] * 5,
        out_specs=anywhere,
        scratch_shapes=[
            pltpu.VMEM((piece, wide), F32),
            pltpu.VMEM((deep, wide), BF16),
            pltpu.VMEM(radiation.shape, BF16),
            pltpu.VMEM((n_near, 2 * block, block), BF16),
            pltpu.VMEM((n_near, 2 * block, block), BF16),
            pltpu.VMEM((stages, block, block), F32),
            pltpu.VMEM((2, 4, rank_most, block), F32),
            pltpu.VMEM((n_far, 2 * block, 2 * rank_pad), BF16),
            pltpu.VMEM((2, n_far, 2 * rank_pad, block), BF16),
            pltpu.VMEM((wide, deep), BF16),
            pltpu.VMEM((wide, piece), F32),
            pltpu.VMEM((wide, block), F32),
            pltpu.VMEM((n_dir - 1, wide, block), F32),
            pltpu.VMEM((n_col, wide, block), F32),
            pltpu.VMEM((n_col, 2 * most, 2 * block), BF16),
            pltpu.VMEM((n_near + n_far, most, block), F32),
            pltpu.VMEM((n_dir, n_row, wide, piece), F32),
            pltpu.VMEM((n_dir - 1, n_row, wide, piece), F32),
            pltpu.VMEM((n_row - 1, wide, piece), F32),
            pltpu.VMEM((n_row, n_dir, plan.row_total, piece), F32),
            pltpu.VMEM((n_row // 2, n_dir, plan.row_total, piece), F32),
            pltpu.VMEM((n_dir - 1, plan.row_total, piece), F32),
            dma((3,)),
            dma((stages,)),
            dma((2, 4)),
            dma((chunks, n_dir - 1)),
            dma((chunks, n_dir - 1)),
            dma((chunks, n_x - 1)),
            dma((chunks, n_x - 1)),
            dma((chunks, n_x)),
            dma((chunks, n_x)),
            dma((chunks, n_dir - 1, n_row)),
            dma((chunks, n_dir - 1, n_row)),
            dma((chunks, n_row)),
            dma((chunks, n_row)),
            dma((chunks, n_row, n_dir)),
            dma((chunks, n_row, n_dir)),
            dma((chunks, n_row // 2, n_dir)),
            dma((chunks, n_dir - 1)),
            dma((chunks, n_dir - 1)),
            dma((4,)),
        ],
        compiler_params=pltpu.CompilerParams(
            collective_id=0, has_side_effects=True, vmem_limit_bytes=67043328
        ),
    )(near_pairs.T, far_pairs.T, far_ranks, block_counts, cotangent, radiation, near_z, far_ut, far_vt)


def solution(mesh):
    return jax.shard_map(
        shards,
        mesh=mesh,
        in_specs=(
            P("dir", None),
            P(None, ("row", "col"), "dir"),
            P(None, ("dir", "row", "col"), None, None),
            P(("dir", "row", "col"), None),
            P(None, ("dir", "row", "col"), None, None),
            P(None, ("dir", "row", "col"), None, None),
            P(("dir", "row", "col"), None),
            P(("dir", "row", "col")),
            P(("dir", "row", "col"), None),
        ),
        out_specs=P(("col", "dir", "row"), None),
        check_vma=False,
    )
```

time: 104 us -> 87.9 us (0.85)
  Pallas kernels: 99.1 us -> 85.3 us
  local copies, waits for them, and re-layouts: 4.56 us -> 1.87 us
    pallas_call x1, Pallas kernels: 99.1 us -> 85.3 us  [shards(): pl.pallas_call(functools.partial(kernel, n_dir, n_row, n_col, plan), out_...]
    unnamed x3 -> x1, local copies, waits for them, and re-layouts: 4.56 us -> 1.87 us
where the time goes in v1:
time: 87.9 us; the launch traced here: 87.1 us
  Pallas kernels  85.3 us (97%)
  local copies, waits for them, and re-layouts  1.87 us (2%)
    pallas_call x1, Pallas kernels, shards(): pl.pallas_call(functools.partial(kernel, n_dir, n_row, n_col, plan), out_...  85.3 us
    unnamed x1, local copies, waits for them, and re-layouts  1.87 us

profile of v1, /device:TPU:0, one launch (start us, length us, event | category | flops | bytes accessed | tf_op | source)
XLA Modules:
  0.0 87.1 jit_solution(9200410395637174120)
XLA Ops:
  0.0 85.3 %shard_map.91 = f32[256,512]{1,0:T(8,128)} custom-call(s32[2,8]{1,0:T(2,128)} %bitcast.2, s32[2,4]{1,0:T(2,128)} %bitcast.3, s32[4]{0:T(128)} %far_ranks.1, s32[1,2]{1,0:T(1,128)} %counts.1, bf16[1024,512]{1,0:T(8,128)(2,1)} %cot_hbm.1, bf16[2,512,1024]{2,1,0:T(8,128)(2,1)} %rad_hbm.1, f32[2,8,512,512]{3,2,1,0:T(8,128)} %near_z.1, f32[2,4,96,512]{3,2,1,0:T(8,128)} %far_ut.1, ...), custom_call_target="tpu_custom_call" | custom-call | tf_op jit(solution)/shard_map/pallas_call | solution.py:496
  85.3 1.9 %copy.11 = f32[256,512]{1,0:T(8,128)} copy(f32[256,512]{1,0:T(8,128)} %shard_map.91) | data formatting | bytes 1048576

commit v2 on v1

--- a/solution.py
+++ b/solution.py
@@ -14,7 +14,23 @@
 NT = (((1,), (1,)), ((), ()))
 PARTS = 8
 SIZES = (1, 1, 2, 2, 2)
-ROW_FIRST = (1.0, 0.0, 0.5, 0.0, 0.0)
+ROW_FIRST = (0.875, 0.5, 0.5, 0, 0.125)
+STEPS = 4
+ORDER = (
+    ("convert", 0), ("convert", 1), ("dirs", 0), ("convert", 2), ("convert", 3), ("pack",), ("dirs", 1), ("relay", 0),
+    ("sides", 0), ("near", 0, 0), ("near", 0, 1), ("near", 0, 2), ("dirs", 2), ("relay", 1), ("near", 0, 3),
+    ("sums", 0), ("sides", 1), ("near", 1, 0), ("near", 1, 1), ("near", 1, 2), ("dirs", 3), ("near", 1, 3),
+    ("sums", 1), ("relay", 2), ("pairs", 0), ("sides", 2), ("near", 2, 0), ("near", 2, 1), ("dirs", 4),
+    ("part", 0, 0), ("part", 0, 1), ("part", 0, 2), ("part", 0, 3), ("near", 2, 2), ("relay", 3), ("part", 1, 0),
+    ("part", 1, 1), ("near", 2, 3), ("pairs", 1), ("part", 1, 2), ("far", 0, 0), ("far", 0, 1), ("part", 1, 3),
+    ("sums", 2), ("rows", 0), ("far", 1, 0), ("sides", 3), ("far", 1, 1), ("near", 3, 0), ("near", 3, 1),
+    ("part", 2, 0), ("near", 3, 2), ("relay", 4), ("rows", 1), ("part", 2, 1), ("near", 3, 3), ("part", 2, 2),
+    ("sums", 3), ("part", 2, 3), ("sides", 4), ("near", 4, 0), ("near", 4, 1), ("pairs", 2), ("near", 4, 2),
+    ("near", 4, 3), ("part", 3, 0), ("far", 2, 0), ("sums", 4), ("far", 2, 1), ("last", 0), ("end", 0), ("last", 1),
+    ("end", 1), ("part", 3, 1), ("rows", 2), ("part", 3, 2), ("far", 3, 0), ("pairs", 4), ("last", 2), ("part", 3, 3),
+    ("far", 3, 1), ("part", 4, 0), ("part", 4, 1), ("rows", 4), ("last", 3), ("part", 4, 2), ("far", 4, 0),
+    ("part", 4, 3), ("far", 4, 1), ("end", 2), ("end", 4), ("last", 4),
+)
 
 
 def dot(left, right):
@@ -41,16 +57,18 @@
 
 
 class Plan:
-    def __init__(self, wide, n_row):
+    def __init__(self, wide, small):
         unit = wide // 2 // PARTS
         self.half = [unit * size for size in SIZES]
         self.width = [2 * half for half in self.half]
         self.first = [sum(self.half[:k]) for k in range(len(self.half))]
         self.row_wide = [int(width * share) for width, share in zip(self.width, ROW_FIRST)]
+        if not small:
+            self.row_wide = [min(8, rows) for rows in self.row_wide]
         self.row_at = [sum(self.row_wide[:k]) for k in range(len(self.half))]
         self.row_total = max(8, sum(self.row_wide))
+        self.dir_total = sum(self.width) - sum(self.row_wide)
         self.chunks = len(self.half)
-        self.offsets = sorted(range(1, n_row), key=lambda o: -min(o, n_row - o)) + [0]
 
     def rows(self, k):
         return slice(2 * self.first[k], 2 * self.first[k] + self.width[k])
@@ -72,9 +90,9 @@
     near_pairs, far_pairs, far_ranks, counts, cot_hbm, rad_hbm, near_z, far_ut, far_vt,
     out,
     placed, cot, rad, z_high, z_low, stage, far_stage, left_far, right_far, cot_t, totals, sent, dir_in, gathered, sides, terms,
-    parts, dir_parts, row_parts, pair_in, row_in, last_in,
-    in_sem, stage_sem, far_sem, d_send, d_recv, x_send, x_recv, c_send, c_recv, p_send, p_recv, r_send, r_recv,
-    a_recv, q_send, q_recv, l_send, l_recv, o_sem,
+    parts, dir_parts, pair_dir, row_dir, pair_in, row_in, last_in,
+    in_sem, stage_sem, far_sem, d_send, d_recv, x_send, x_recv, c_send, c_recv, p_send, p_recv, r_send, f_recv, r_recv,
+    q_send, a_recv, q_recv, l_send, l_recv, o_sem,
 ):
     chunks = plan.chunks
     wide = cot.shape[1]
@@ -85,7 +103,7 @@
     piece = block // n_dir
     n_x = n_col // CORES
     per_dir = n_row // n_dir
-    n_off = len(plan.offsets)
+    n_cross, own = n_row - 2, n_row - 1
     d = lax.axis_index("dir")
     r = lax.axis_index("row")
     c = lax.axis_index("col")
@@ -99,8 +117,17 @@
     def x_peer(j):
         return (d, r, lax.rem(x + j, n_x) * CORES + core)
 
+    def row_of(i):
+        base = 2 * (r // 2)
+        if i < n_cross:
+            return jnp.where(r < n_row // 2, lax.rem(base + n_row - 1 - i, n_row), lax.rem(base + 2 + i, n_row))
+        return row_pair if i == n_cross else r
+
     def row_peer(i):
-        return (d, lax.rem(r + plan.offsets[i], n_row), c)
+        return (d, row_of(i), c)
+
+    def gathers(i):
+        return (row_of(i) > r) == (lax.rem(r, 2) == 1)
 
     def from_x(j, core_of):
         return lax.rem(x + n_x - j, n_x) * CORES + core_of
@@ -112,7 +139,7 @@
 
     peers = [dir_peer(j) for j in range(1, n_dir)]
     peers += [x_peer(j) for j in range(1, n_x)]
-    peers += [row_peer(i) for i in range(n_off - 1)]
+    peers += [row_peer(i) for i in range(own)]
     peers.append((d, r, partner))
     barrier = pltpu.get_barrier_semaphore()
     for device in peers:
@@ -139,60 +166,53 @@
 
     def send_dir(k, j):
         rows = plan.rows(k)
-        return remote(sent.at[rows], dir_in.at[j - 1, rows], d_send.at[k, j - 1], d_recv.at[k, j - 1], dir_peer(j))
+        return remote(sent.at[rows], dir_in.at[j - 1, rows], d_send.at[j - 1], d_recv.at[k, j - 1], dir_peer(j))
 
     def send_x(k, j, which=None):
         block_of = gathered.at[c if which is None else which, plan.rows(k)]
-        return remote(block_of, block_of, x_send.at[k, j - 1], x_recv.at[k, j - 1], x_peer(j))
+        return remote(block_of, block_of, x_send.at[j - 1], x_recv.at[k, j - 1], x_peer(j))
 
     def send_core(k, j, core_of):
         block_of = gathered.at[from_x(j, core_of), plan.rows(k)]
-        return remote(block_of, block_of, c_send.at[k, j], c_recv.at[k, j], (d, r, partner))
+        return remote(block_of, block_of, c_send.at[0], c_recv.at[k, j], (d, r, partner))
 
     def send_part(k, j, i):
         rows = plan.dir_rows(k)
         return remote(
-            parts.at[j, i, rows], dir_parts.at[j - 1, i, rows], p_send.at[k, j - 1, i], p_recv.at[k, j - 1, i], dir_peer(j)
+            parts.at[j, i, rows], dir_parts.at[j - 1, i, rows], p_send.at[0], p_recv.at[k, j - 1, i], dir_peer(j)
         )
 
-    def send_row(k, i):
+    def pair_part(k, i):
         rows = plan.dir_rows(k)
-        return remote(parts.at[0, i, rows], row_parts.at[i, rows], r_send.at[k, i], r_recv.at[k, i], row_peer(i))
-
-    def row_of(i):
-        return lax.rem(r + plan.offsets[i], n_row)
-
-    def same_pair(i):
-        return row_of(i) // 2 == r // 2
-
-    def gathers(i):
-        above = row_of(i) > r
-        odd = lax.rem(r, 2) == 1
-        return jnp.logical_not(same_pair(i)) & (above == odd)
+        return remote(parts.at[0, i, rows], pair_dir.at[i, rows], r_send.at[0], f_recv.at[k, i], row_peer(n_cross))
+
+    def send_row(k, i, p):
+        rows = plan.dir_rows(k)
+        return remote(parts.at[0, i, rows], row_dir.at[p, rows], r_send.at[0], r_recv.at[k, p], row_peer(i))
 
     def send_pair(k, i, j):
         return remote(
             parts.at[j, i, plan.row_rows(k)],
-            pair_in.at[row_of(i), j, plan.row_slots(k)],
-            q_send.at[k, i, j],
-            a_recv.at[k, row_of(i), j],
-            (d, row_pair, c),
+            pair_in.at[i, j, plan.row_slots(k)],
+            q_send.at[0],
+            a_recv.at[k, i],
+            row_peer(n_cross),
         )
 
     def send_sum(k, i, j):
         return remote(
             parts.at[j, i, plan.row_rows(k)],
             row_in.at[r // 2, j, plan.row_slots(k)],
-            q_send.at[k, i, j],
-            q_recv.at[k, r // 2, j],
+            q_send.at[0],
+            q_recv.at[k, r // 2],
             row_peer(i),
         )
 
     def send_last(k, j):
         return remote(
-            parts.at[j, n_off - 1, plan.row_rows(k)],
+            parts.at[j, own, plan.row_rows(k)],
             last_in.at[j - 1, plan.row_slots(k)],
-            l_send.at[k, j - 1],
+            l_send.at[0],
             l_recv.at[k, j - 1],
             dir_peer(j),
         )
@@ -263,8 +283,9 @@
             send_x(k, j, from_x(j, core)).wait_recv()
             send_core(k, j, core).start()
 
-    def products(k, between=None):
-        between = {min(stop, n_far): calls for stop, calls in (between or {}).items()}
+    per_far = n_near // n_far
+
+    def make_sides(k):
         width, rows = plan.width[k], plan.rows(k)
         for j in range(n_x):
             send_core(k, j, CORES - 1 - core).wait_recv()
@@ -278,13 +299,14 @@
 
         lax.fori_loop(0, n_col, side, 0)
 
-        per_far = n_near // n_far
+    def multiply(k, step):
+        width = plan.width[k]
 
         def near(s):
             left = sides[lax.rem(near_pairs[0, s], n_col), : 2 * width]
             terms[s, :width] = fold(dot(left, z_high[s])) + dot(left[:width], z_low[s])
 
-        def body(s, carry):
+        def body(s):
             both = dot(sides[lax.rem(far_pairs[0, s], n_col), : 2 * width], left_far[s])
             near(s * per_far)
             coeffs = fold(both[:, :rank_pad]) + both[:width, rank_pad:]
@@ -295,18 +317,14 @@
                 near(s * per_far + i)
             both = dot(jnp.concatenate([high, low], axis=0), right_far[0, s])
             terms[n_near + s, :width] = fold(both) + dot(high, right_far[1, s])
-            return carry
-
-        at = 0
-        for stop in sorted({*between, n_far}):
-            if stop > at:
-                lax.fori_loop(at, stop, body, 0)
-            at = stop
-            for call, i in between.pop(stop, ()):
-                call(i)
-
+
+        for s in range(n_far * step // STEPS, n_far * (step + 1) // STEPS):
+            body(s)
+
+    def make_sums(k):
+        width, rows = plan.width[k], plan.rows(k)
         for j in list(range(1, n_dir)) + [0]:
-            for i in range(n_off):
+            for i in range(n_row):
                 q = row_of(i)
                 target = c * n_row + lax.rem(d + j, n_dir) * per_dir + q // n_dir
                 lanes = pl.ds(pl.multiple_of(lax.rem(q, n_dir) * piece, piece), piece)
@@ -319,56 +337,64 @@
                 parts[j, i, rows] = total
                 if j > 0 and plan.row_wide[k] < width:
                     send_part(k, j, i).start()
-                if i < n_off - 1 and plan.row_wide[k] > 0:
-                    own = same_pair(i)
-                    mine = gathers(i)
-
-                    @pl.when(own)
-                    def _():
-                        send_sum(k, i, j).start()
-
-                    @pl.when(jnp.logical_not(own | mine))
+                if i == n_cross and plan.row_wide[k] > 0:
+                    send_sum(k, i, j).start()
+                if i < n_cross and plan.row_wide[k] > 0:
+
+                    @pl.when(jnp.logical_not(gathers(i)))
                     def _():
                         send_pair(k, i, j).start()
 
-    def add_parts(k, first=0, last=n_off):
-        if plan.row_wide[k] == plan.width[k]:
-            return
+    def add_part(k, step):
         rows = plan.dir_rows(k)
-        for i in range(first, last):
+        for i in range(n_row * step // STEPS, n_row * (step + 1) // STEPS):
             total = parts[0, i, rows]
             for j in range(1, n_dir):
                 send_part(k, j, i).wait_recv()
                 total = total + dir_parts[j - 1, i, rows]
             parts[0, i, rows] = total
-            if i < n_off - 1:
-                send_row(k, i).start()
+            if i == n_cross:
+                send_row(k, i, r // 2).start()
+            if i < n_cross:
+
+                @pl.when(jnp.logical_not(gathers(i)))
+                def _():
+                    pair_part(k, i).start()
+
+    def add_far(k, step):
+        rows = plan.dir_rows(k)
+        for i in range(n_row * step // STEPS, min(n_cross, n_row * (step + 1) // STEPS)):
+
+            @pl.when(gathers(i))
+            def _():
+                pair_part(k, i).wait_recv()
+                parts[0, i, rows] = parts[0, i, rows] + pair_dir[i, rows]
+                send_row(k, i, r // 2).start()
 
     def add_pairs(k):
-        if plan.row_wide[k] == 0:
-            return
         rows, slots = plan.row_rows(k), plan.row_slots(k)
+        for i in range(n_cross):
+
+            @pl.when(gathers(i))
+            def _():
+                remote(
+                    parts.at[:, i, rows], pair_in.at[i, :, slots], q_send.at[0], a_recv.at[k, i], row_peer(n_cross)
+                ).wait_recv()
+                for j in list(range(1, n_dir)) + [0]:
+                    parts[j, i, rows] = parts[j, i, rows] + pair_in[i, j, slots]
+                    send_sum(k, i, j).start()
+
+    def add_rows(k):
+        rows, slots = plan.row_rows(k), plan.row_slots(k)
+        for p in range(n_row // 2):
+            remote(
+                parts.at[:, own, rows], row_in.at[p, :, slots], q_send.at[0], q_recv.at[k, p], row_peer(n_cross)
+            ).wait_recv()
         for j in list(range(1, n_dir)) + [0]:
-            for i in range(n_off - 1):
-
-                @pl.when(gathers(i))
-                def _():
-                    send_pair(k, i, j).wait_recv()
-                    parts[j, i, rows] = parts[j, i, rows] + pair_in[row_of(i), j, slots]
-                    send_sum(k, i, j).start()
-
-    def add_rows(k):
-        if plan.row_wide[k] == 0:
-            return
-        rows, slots = plan.row_rows(k), plan.row_slots(k)
-        for j in list(range(1, n_dir)) + [0]:
-            total = parts[j, n_off - 1, rows]
+            total = parts[j, own, rows]
             for p in range(n_row // 2):
-                remote(
-                    parts.at[j, n_off - 1, rows], row_in.at[p, j, slots], l_send.at[k, 0], q_recv.at[k, p, j], row_peer(0)
-                ).wait_recv()
                 total = total + row_in[p, j, slots]
-            parts[j, n_off - 1, rows] = total
+            parts[j, own, rows] = total
             if j > 0:
                 send_last(k, j).start()
 
@@ -384,20 +410,16 @@
             totals[base + cut : base + stop] = total[cut - start :]
 
     def finish_dir(k):
-        if plan.row_wide[k] == plan.width[k]:
-            return
         rows = plan.dir_rows(k)
-        total = parts[0, n_off - 1, rows]
-        for i in range(n_off - 1):
-            send_row(k, i).wait_recv()
-            total = total + row_parts[i, rows]
+        total = parts[0, own, rows]
+        for p in range(n_row // 2):
+            send_row(k, own, p).wait_recv()
+            total = total + row_dir[p, rows]
         place(k, 0, total)
 
     def finish_row(k):
-        if plan.row_wide[k] == 0:
-            return
         rows, slots = plan.row_rows(k), plan.row_slots(k)
-        total = parts[0, n_off - 1, rows]
+        total = parts[0, own, rows]
         for j in range(1, n_dir):
             send_last(k, j).wait_recv()
             total = total + last_in[j - 1, slots]
@@ -412,25 +434,23 @@
             put_copies.append(copy)
 
     def drain():
-        for k in range(chunks):
-            for j in range(1, n_dir):
-                send_dir(k, j).wait_send()
-            for j in range(1, n_x):
-                send_x(k, j).wait_send()
-            for j in range(n_x):
-                send_core(k, j, core).wait_send()
-            if plan.row_wide[k] < plan.width[k]:
-                for i in range(n_off):
-                    for j in range(1, n_dir):
-                        send_part(k, j, i).wait_send()
-                    if i < n_off - 1:
-                        send_row(k, i).wait_send()
-            if plan.row_wide[k] > 0:
-                for j in range(n_dir):
-                    for i in range(n_off - 1):
-                        send_sum(k, i, j).wait_send()
-                    if j > 0:
-                        send_last(k, j).wait_send()
+        for j in range(1, n_dir):
+            remote(sent, dir_in.at[j - 1], d_send.at[j - 1], d_recv.at[0, 0], dir_peer(1)).wait_send()
+        for j in range(1, n_x):
+            remote(gathered.at[0], gathered.at[0], x_send.at[j - 1], x_recv.at[0, 0], x_peer(1)).wait_send()
+        all_of = gathered.at[pl.ds(0, n_x)]
+        remote(all_of, all_of, c_send.at[0], c_recv.at[0, 0], (d, r, partner)).wait_send()
+        dir_rows, row_rows = pl.ds(0, plan.dir_total), pl.ds(0, sum(plan.row_wide))
+        if plan.dir_total > 0:
+            all_of = parts.at[pl.ds(1, n_dir - 1), :, dir_rows]
+            remote(all_of, all_of, p_send.at[0], p_recv.at[0, 0, 0], dir_peer(1)).wait_send()
+            all_of = parts.at[0, pl.ds(0, own), dir_rows]
+            remote(all_of, all_of, r_send.at[0], r_recv.at[0, 0], row_peer(n_cross)).wait_send()
+        if sum(plan.row_wide) > 0:
+            all_of = parts.at[:, pl.ds(0, own), row_rows]
+            remote(all_of, all_of, q_send.at[0], q_recv.at[0, 0], row_peer(n_cross)).wait_send()
+            all_of = parts.at[pl.ds(1, n_dir - 1), own, row_rows]
+            remote(all_of, all_of, l_send.at[0], l_recv.at[0, 0], dir_peer(1)).wait_send()
         for copy in put_copies:
             copy.wait()
 
@@ -452,27 +472,37 @@
             for j in range(1, n_dir):
                 send_dir(i, j).start()
 
-    convert(0, n_near)
-    add_dirs(0)
-    pack_far()
-    add_dirs(1)
-    relay(0)
-    products(0, {2: [(relay, 1), (add_dirs, 2)]})
-    products(1, {2: [(add_dirs, 3)], 4: [(relay, 2)]})
-    products(2, {1: [(add_pairs, 0)], 2: [(add_dirs, 4)], 4: [(relay, 3)]})
-    products(3, {1: [(add_rows, 0)], 2: [(add_parts, 1)], 4: [(relay, 4)]})
-    products(4, {1: [(add_pairs, 2)], 3: [(add_parts, 2)]})
-    add_rows(2)
-    finish_row(0)
-    finish_dir(1)
-    add_parts(3)
-    finish_dir(2)
-    add_parts(4)
-    finish_row(2)
-    put(0, plan.first[3])
-    finish_dir(3)
-    finish_dir(4)
-    put(plan.first[3], wide // 2)
+    waiting = {k: (plan.row_wide[k] > 0) + (plan.row_wide[k] < plan.width[k]) for k in range(chunks)}
+    put_at = [0]
+
+    def finished(k):
+        waiting[k] -= 1
+        ends = [stop for stop in range(128, wide // 2 + 1, 128) if stop > put_at[0]]
+        for stop in ends:
+            if any(waiting[i] for i in range(chunks) if plan.first[i] < stop):
+                return
+            put(put_at[0], stop)
+            put_at[0] = stop
+
+    calls = {
+        "convert": lambda i: convert(n_near * i // STEPS, n_near * (i + 1) // STEPS),
+        "pack": pack_far,
+        "dirs": add_dirs,
+        "relay": relay,
+        "sides": make_sides,
+        "near": multiply,
+        "sums": make_sums,
+        "part": add_part,
+        "far": add_far,
+        "pairs": add_pairs,
+        "rows": add_rows,
+        "last": finish_dir,
+        "end": finish_row,
+    }
+    for name, *at in ORDER:
+        calls[name](*at)
+        if name in ("last", "end"):
+            finished(at[0])
     drain()
 
 
@@ -481,13 +511,13 @@
 ):
     n_dir, n_row, n_col = (lax.axis_size(name) for name in ("dir", "row", "col"))
     deep, wide = cotangent.shape
-    plan = Plan(wide, n_row)
+    small = n_row * n_col <= 16
+    plan = Plan(wide, small)
     chunks, most = plan.chunks, max(plan.width)
     block = near_z.shape[2]
     n_near, n_far, rank_most = near_z.shape[1], far_ut.shape[1], far_ut.shape[2]
     n_x = n_col // CORES
     piece = block // n_dir
-    small = n_row * n_col <= 16
     stages = min(6 if small else 2, 2 * n_near)
     rank_pad = -(-rank_most // 128) * 128
     smem = pl.BlockSpec(memory_space=pltpu.SMEM)
@@ -517,27 +547,29 @@
             pltpu.VMEM((n_near + n_far, most, block), F32),
             pltpu.VMEM((n_dir, n_row, wide, piece), F32),
             pltpu.VMEM((n_dir - 1, n_row, wide, piece), F32),
-            pltpu.VMEM((n_row - 1, wide, piece), F32),
-            pltpu.VMEM((n_row, n_dir, plan.row_total, piece), F32),
+            pltpu.VMEM((n_row - 2, wide, piece), F32),
+            pltpu.VMEM((n_row // 2, wide, piece), F32),
+            pltpu.VMEM((n_row - 2, n_dir, plan.row_total, piece), F32),
             pltpu.VMEM((n_row // 2, n_dir, plan.row_total, piece), F32),
             pltpu.VMEM((n_dir - 1, plan.row_total, piece), F32),
             dma((3,)),
             dma((stages,)),
             dma((2, 4)),
+            dma((n_dir - 1,)),
             dma((chunks, n_dir - 1)),
-            dma((chunks, n_dir - 1)),
+            dma((n_x - 1,)),
             dma((chunks, n_x - 1)),
-            dma((chunks, n_x - 1)),
+            dma((1,)),
             dma((chunks, n_x)),
-            dma((chunks, n_x)),
+            dma((1,)),
             dma((chunks, n_dir - 1, n_row)),
-            dma((chunks, n_dir - 1, n_row)),
-            dma((chunks, n_row)),
-            dma((chunks, n_row)),
-            dma((chunks, n_row, n_dir)),
-            dma((chunks, n_row, n_dir)),
-            dma((chunks, n_row // 2, n_dir)),
-            dma((chunks, n_dir - 1)),
+            dma((1,)),
+            dma((chunks, n_row - 2)),
+            dma((chunks, n_row // 2)),
+            dma((1,)),
+            dma((chunks, n_row - 2)),
+            dma((chunks, n_row // 2)),
+            dma((1,)),
             dma((chunks, n_dir - 1)),
             dma((4,)),
         ],

time: 87.9 us -> 74.4 us (0.85)
  Pallas kernels: 85.3 us -> 72.3 us
    pallas_call x1, Pallas kernels: 85.3 us -> 72.3 us  [shards(): pl.pallas_call(functools.partial(kernel, n_dir, n_row, n_col, plan), out_...]
where the time goes in v2:
time: 74.4 us; the launch traced here: 74.2 us
  Pallas kernels  72.3 us (97%)
  local copies, waits for them, and re-layouts  1.87 us (3%)
    pallas_call x1, Pallas kernels, shards(): pl.pallas_call(functools.partial(kernel, n_dir, n_row, n_col, plan), out_...  72.3 us
    unnamed x1, local copies, waits for them, and re-layouts  1.87 us

profile of v2, /device:TPU:0, one launch (start us, length us, event | category | flops | bytes accessed | tf_op | source)
XLA Modules:
  0.0 74.2 jit_solution(13066380024038199503)
XLA Ops:
  0.0 72.3 %shard_map.91 = f32[256,512]{1,0:T(8,128)} custom-call(s32[2,8]{1,0:T(2,128)} %bitcast.2, s32[2,4]{1,0:T(2,128)} %bitcast.3, s32[4]{0:T(128)} %far_ranks.1, s32[1,2]{1,0:T(1,128)} %counts.1, bf16[1024,512]{1,0:T(8,128)(2,1)} %cot_hbm.1, bf16[2,512,1024]{2,1,0:T(8,128)(2,1)} %rad_hbm.1, f32[2,8,512,512]{3,2,1,0:T(8,128)} %near_z.1, f32[2,4,96,512]{3,2,1,0:T(8,128)} %far_ut.1, ...), custom_call_target="tpu_custom_call" | custom-call | tf_op jit(solution)/shard_map/pallas_call | solution.py:526
  72.3 1.9 %copy.11 = f32[256,512]{1,0:T(8,128)} copy(f32[256,512]{1,0:T(8,128)} %shard_map.91) | data formatting | bytes 1048576

commit v3 on v2

--- a/solution.py
+++ b/solution.py
@@ -14,22 +14,22 @@
 NT = (((1,), (1,)), ((), ()))
 PARTS = 8
 SIZES = (1, 1, 2, 2, 2)
-ROW_FIRST = (0.875, 0.5, 0.5, 0, 0.125)
+ROW_FIRST = (0.625, 0.75, 0.5, 0, 0)
 STEPS = 4
 ORDER = (
-    ("convert", 0), ("convert", 1), ("dirs", 0), ("convert", 2), ("convert", 3), ("pack",), ("dirs", 1), ("relay", 0),
-    ("sides", 0), ("near", 0, 0), ("near", 0, 1), ("near", 0, 2), ("dirs", 2), ("relay", 1), ("near", 0, 3),
-    ("sums", 0), ("sides", 1), ("near", 1, 0), ("near", 1, 1), ("near", 1, 2), ("dirs", 3), ("near", 1, 3),
-    ("sums", 1), ("relay", 2), ("pairs", 0), ("sides", 2), ("near", 2, 0), ("near", 2, 1), ("dirs", 4),
-    ("part", 0, 0), ("part", 0, 1), ("part", 0, 2), ("part", 0, 3), ("near", 2, 2), ("relay", 3), ("part", 1, 0),
-    ("part", 1, 1), ("near", 2, 3), ("pairs", 1), ("part", 1, 2), ("far", 0, 0), ("far", 0, 1), ("part", 1, 3),
-    ("sums", 2), ("rows", 0), ("far", 1, 0), ("sides", 3), ("far", 1, 1), ("near", 3, 0), ("near", 3, 1),
-    ("part", 2, 0), ("near", 3, 2), ("relay", 4), ("rows", 1), ("part", 2, 1), ("near", 3, 3), ("part", 2, 2),
+    ("convert", 0), ("convert", 1), ("convert", 2), ("dirs", 0), ("convert", 3), ("pack",), ("dirs", 1), ("relay", 0),
+    ("sides", 0), ("near", 0, 0), ("near", 0, 1), ("relay", 1), ("near", 0, 2), ("dirs", 2), ("near", 0, 3),
+    ("sums", 0), ("sides", 1), ("near", 1, 0), ("near", 1, 1), ("near", 1, 2), ("near", 1, 3), ("sums", 1),
+    ("dirs", 3), ("pairs", 0), ("relay", 2), ("sides", 2), ("near", 2, 0), ("near", 2, 1), ("dirs", 4),
+    ("near", 2, 2), ("relay", 3), ("rows", 0), ("part", 0, 0), ("part", 0, 1), ("part", 0, 2), ("pairs", 1),
+    ("near", 2, 3), ("part", 0, 3), ("part", 1, 0), ("part", 1, 1), ("part", 1, 2), ("sums", 2), ("far", 0, 0),
+    ("part", 1, 3), ("far", 0, 1), ("sides", 3), ("near", 3, 0), ("far", 1, 0), ("far", 1, 1), ("near", 3, 1),
+    ("part", 2, 0), ("near", 3, 2), ("relay", 4), ("part", 2, 1), ("rows", 1), ("near", 3, 3), ("part", 2, 2),
     ("sums", 3), ("part", 2, 3), ("sides", 4), ("near", 4, 0), ("near", 4, 1), ("pairs", 2), ("near", 4, 2),
-    ("near", 4, 3), ("part", 3, 0), ("far", 2, 0), ("sums", 4), ("far", 2, 1), ("last", 0), ("end", 0), ("last", 1),
-    ("end", 1), ("part", 3, 1), ("rows", 2), ("part", 3, 2), ("far", 3, 0), ("pairs", 4), ("last", 2), ("part", 3, 3),
-    ("far", 3, 1), ("part", 4, 0), ("part", 4, 1), ("rows", 4), ("last", 3), ("part", 4, 2), ("far", 4, 0),
-    ("part", 4, 3), ("far", 4, 1), ("end", 2), ("end", 4), ("last", 4),
+    ("part", 3, 0), ("near", 4, 3), ("far", 2, 0), ("sums", 4), ("far", 2, 1), ("part", 3, 1), ("end", 0),
+    ("last", 0), ("last", 1), ("end", 1), ("part", 3, 2), ("rows", 2), ("far", 3, 0), ("part", 3, 3), ("last", 2),
+    ("far", 3, 1), ("part", 4, 0), ("part", 4, 1), ("last", 3), ("far", 4, 0), ("part", 4, 2), ("far", 4, 1),
+    ("part", 4, 3), ("end", 2), ("last", 4),
 )
 
 
@@ -89,10 +89,10 @@
     n_dir, n_row, n_col, plan,
     near_pairs, far_pairs, far_ranks, counts, cot_hbm, rad_hbm, near_z, far_ut, far_vt,
     out,
-    placed, cot, rad, z_high, z_low, stage, far_stage, left_far, right_far, cot_t, totals, sent, dir_in, gathered, sides, terms,
+    cot, rad, z_high, z_low, stage, far_stage, left_far, right_far, cot_t, totals, sent, dir_in, gathered, sides, terms,
     parts, dir_parts, pair_dir, row_dir, pair_in, row_in, last_in,
     in_sem, stage_sem, far_sem, d_send, d_recv, x_send, x_recv, c_send, c_recv, p_send, p_recv, r_send, f_recv, r_recv,
-    q_send, a_recv, q_recv, l_send, l_recv, o_sem,
+    q_send, a_recv, q_recv, l_send, l_recv,
 ):
     chunks = plan.chunks
     wide = cot.shape[1]
@@ -217,10 +217,16 @@
             dir_peer(j),
         )
 
-    def right_sides(k):
-        at, half = plan.first[k], plan.half[k]
-        left = jnp.concatenate([cot_t[at : at + half], cot_t[wide // 2 + at : wide // 2 + at + half]], axis=0)
-        sent[plan.rows(k)] = dot_nt(left, rad[0]) + dot_nt(swap_rows(left), rad[1])
+    def right_sides(first, last):
+        at, stop = plan.first[first], plan.first[last] + plan.half[last]
+        half = stop - at
+        left = jnp.concatenate([cot_t[at:stop], cot_t[wide // 2 + at : wide // 2 + stop]], axis=0)
+        result = dot_nt(left, rad[0]) + dot_nt(swap_rows(left), rad[1])
+        for k in range(first, last + 1):
+            base, size = plan.first[k] - at, plan.half[k]
+            rows = plan.rows(k)
+            sent[rows.start : rows.start + size] = result[base : base + size]
+            sent[rows.start + size : rows.stop] = result[half + base : half + base + size]
 
     def convert(first, last):
         def body(item, carry):
@@ -428,10 +434,7 @@
     def put(first, last):
         for base in (0, wide // 2):
             columns = slice(base + first, base + last)
-            placed[:, columns] = totals[columns].T
-            copy = pltpu.make_async_copy(placed.at[:, columns], out.at[:, columns], o_sem.at[len(put_copies)])
-            copy.start()
-            put_copies.append(copy)
+            out[:, columns] = totals[columns].T
 
     def drain():
         for j in range(1, n_dir):
@@ -451,26 +454,24 @@
             remote(all_of, all_of, q_send.at[0], q_recv.at[0, 0], row_peer(n_cross)).wait_send()
             all_of = parts.at[pl.ds(1, n_dir - 1), own, row_rows]
             remote(all_of, all_of, l_send.at[0], l_recv.at[0, 0], dir_peer(1)).wait_send()
-        for copy in put_copies:
-            copy.wait()
-
-    put_copies = []
-
-    for load in inputs:
+
+    inputs[0].wait()
+    cot_t[...] = cot[...].T
+    for load in inputs[1:]:
         load.wait()
     for item in range(stages):
         load_item(item).start()
     for s in range(min(2, n_far)):
         for load in load_far(s):
             load.start()
-    cot_t[...] = cot[...].T
-    for k in range(chunks):
-        right_sides(k)
-        if k == 1:
+    early = next(k for k in range(chunks) if plan.first[k] + plan.half[k] >= 2 * wide // (2 * PARTS))
+    for group in ((0, early), (early + 1, chunks - 1)):
+        right_sides(*group)
+        if group[0] == 0:
             pl.semaphore_wait(barrier, len(peers))
-        for i in ((0, 1) if k == 1 else (k,) if k > 1 else ()):
+        for k in range(group[0], group[1] + 1):
             for j in range(1, n_dir):
-                send_dir(i, j).start()
+                send_dir(k, j).start()
 
     waiting = {k: (plan.row_wide[k] > 0) + (plan.row_wide[k] < plan.width[k]) for k in range(chunks)}
     put_at = [0]
@@ -525,11 +526,10 @@
     dma = pltpu.SemaphoreType.DMA
     return pl.pallas_call(
         functools.partial(kernel, n_dir, n_row, n_col, plan),
-        out_shape=jax.ShapeDtypeStruct((piece, wide), F32),
+        out_shape=pltpu.VMEM((piece, wide), F32),
         in_specs=[smem] * 4 + [anywhere] * 5,
-        out_specs=anywhere,
+        out_specs=pl.BlockSpec(memory_space=pltpu.VMEM),
         scratch_shapes=[
-            pltpu.VMEM((piece, wide), F32),
             pltpu.VMEM((deep, wide), BF16),
             pltpu.VMEM(radiation.shape, BF16),
             pltpu.VMEM((n_near, 2 * block, block), BF16),
@@ -571,10 +571,9 @@
             dma((chunks, n_row // 2)),
             dma((1,)),
             dma((chunks, n_dir - 1)),
-            dma((4,)),
         ],
         compiler_params=pltpu.CompilerParams(
-            collective_id=0, has_side_effects=True, vmem_limit_bytes=67043328
+            collective_id=0, has_side_effects=True, vmem_limit_bytes=67043328 - 4 * piece * wide
         ),
     )(near_pairs.T, far_pairs.T, far_ranks, block_counts, cotangent, radiation, near_z, far_ut, far_vt)
 

time: 74.4 us -> 71.9 us (0.966)
  Pallas kernels: 72.3 us -> 70.9 us
  local copies, waits for them, and re-layouts: 1.87 us -> 0.8 us
    pallas_call x1, Pallas kernels: 72.3 us -> 70.9 us  [shards(): pl.pallas_call(functools.partial(kernel, n_dir, n_row, n_col, plan), out_...]
    unnamed x1, local copies, waits for them, and re-layouts: 1.87 us -> 0.8 us
where the time goes in v3:
time: 71.9 us; the launch traced here: 71.7 us
  Pallas kernels  70.9 us (99%)
  local copies, waits for them, and re-layouts  0.8 us (1%)
    pallas_call x1, Pallas kernels, shards(): pl.pallas_call(functools.partial(kernel, n_dir, n_row, n_col, plan), out_...  70.9 us

profile of v3, /device:TPU:0, one launch (start us, length us, event | category | flops | bytes accessed | tf_op | source)
XLA Modules:
  0.0 71.7 jit_solution(9795696391134437584)
XLA Ops:
  0.0 70.9 %shard_map.91 = f32[256,512]{1,0:T(8,128)S(1)} custom-call(s32[2,8]{1,0:T(2,128)} %bitcast.2, s32[2,4]{1,0:T(2,128)} %bitcast.3, s32[4]{0:T(128)} %far_ranks.1, s32[1,2]{1,0:T(1,128)} %counts.1, bf16[1024,512]{1,0:T(8,128)(2,1)} %cot_hbm.1, bf16[2,512,1024]{2,1,0:T(8,128)(2,1)} %rad_hbm.1, f32[2,8,512,512]{3,2,1,0:T(8,128)} %near_z.1, ...), custom_call_target="tpu_custom_call" | custom-call | tf_op jit(solution)/shard_map/pallas_call | solution.py:527
  70.9 0.8 %copy.11 = f32[256,512]{1,0:T(8,128)} copy(f32[256,512]{1,0:T(8,128)S(1)} %shard_map.91) | data formatting | bytes 1048576

commit v4 on v3

--- a/solution.py
+++ b/solution.py
@@ -13,23 +13,25 @@
 BF16 = jnp.bfloat16
 NT = (((1,), (1,)), ((), ()))
 PARTS = 8
-SIZES = (1, 1, 2, 2, 2)
-ROW_FIRST = (0.625, 0.75, 0.5, 0, 0)
+SIZES = (1, 1.5, 1.5, 2, 2)
+ROW_FIRST = (0.875, 0.75, 0.25, 0, 0)
+UNITS = (2, 2, 2, 2, 2)
 STEPS = 4
 ORDER = (
-    ("convert", 0), ("convert", 1), ("convert", 2), ("dirs", 0), ("convert", 3), ("pack",), ("dirs", 1), ("relay", 0),
-    ("sides", 0), ("near", 0, 0), ("near", 0, 1), ("relay", 1), ("near", 0, 2), ("dirs", 2), ("near", 0, 3),
-    ("sums", 0), ("sides", 1), ("near", 1, 0), ("near", 1, 1), ("near", 1, 2), ("near", 1, 3), ("sums", 1),
-    ("dirs", 3), ("pairs", 0), ("relay", 2), ("sides", 2), ("near", 2, 0), ("near", 2, 1), ("dirs", 4),
-    ("near", 2, 2), ("relay", 3), ("rows", 0), ("part", 0, 0), ("part", 0, 1), ("part", 0, 2), ("pairs", 1),
-    ("near", 2, 3), ("part", 0, 3), ("part", 1, 0), ("part", 1, 1), ("part", 1, 2), ("sums", 2), ("far", 0, 0),
-    ("part", 1, 3), ("far", 0, 1), ("sides", 3), ("near", 3, 0), ("far", 1, 0), ("far", 1, 1), ("near", 3, 1),
-    ("part", 2, 0), ("near", 3, 2), ("relay", 4), ("part", 2, 1), ("rows", 1), ("near", 3, 3), ("part", 2, 2),
-    ("sums", 3), ("part", 2, 3), ("sides", 4), ("near", 4, 0), ("near", 4, 1), ("pairs", 2), ("near", 4, 2),
-    ("part", 3, 0), ("near", 4, 3), ("far", 2, 0), ("sums", 4), ("far", 2, 1), ("part", 3, 1), ("end", 0),
-    ("last", 0), ("last", 1), ("end", 1), ("part", 3, 2), ("rows", 2), ("far", 3, 0), ("part", 3, 3), ("last", 2),
-    ("far", 3, 1), ("part", 4, 0), ("part", 4, 1), ("last", 3), ("far", 4, 0), ("part", 4, 2), ("far", 4, 1),
-    ("part", 4, 3), ("end", 2), ("last", 4),
+    ("convert", 0), ("convert", 1), ("dirs", 0), ("convert", 2), ("dirs", 1), ("convert", 3), ("pack",), ("dirs", 2),
+    ("relay", 0), ("relay", 1), ("dirs", 3), ("sides", 0), ("near", 0, 0), ("near", 0, 1), ("dirs", 4), ("relay", 2),
+    ("near", 0, 2), ("near", 0, 3), ("dirs", 5), ("relay", 3), ("sums", 0), ("sides", 1), ("near", 1, 0), ("dirs", 6),
+    ("relay", 4), ("near", 1, 1), ("near", 1, 2), ("relay", 5), ("near", 1, 3), ("dirs", 7), ("sums", 1),
+    ("sides", 2), ("relay", 6), ("near", 2, 0), ("dirs", 8), ("pairs", 0), ("near", 2, 1), ("near", 2, 2),
+    ("relay", 7), ("near", 2, 3), ("dirs", 9), ("part", 0, 0), ("part", 0, 1), ("part", 0, 2), ("part", 0, 3),
+    ("sums", 2), ("part", 1, 0), ("sides", 3), ("part", 1, 1), ("near", 3, 0), ("relay", 8), ("part", 1, 2),
+    ("part", 1, 3), ("near", 3, 1), ("rows", 0), ("near", 3, 2), ("relay", 9), ("part", 2, 0), ("near", 3, 3),
+    ("pairs", 1), ("part", 2, 1), ("sums", 3), ("far", 0, 0), ("part", 2, 2), ("far", 0, 1), ("sides", 4),
+    ("near", 4, 0), ("part", 2, 3), ("near", 4, 1), ("pairs", 2), ("near", 4, 2), ("far", 1, 0), ("far", 1, 1),
+    ("near", 4, 3), ("part", 3, 0), ("sums", 4), ("far", 2, 0), ("end", 0), ("rows", 1), ("last", 0), ("far", 2, 1),
+    ("part", 3, 1), ("rows", 2), ("last", 1), ("part", 3, 2), ("far", 3, 0), ("last", 2), ("part", 3, 3),
+    ("far", 3, 1), ("part", 4, 0), ("last", 3), ("part", 4, 1), ("far", 4, 0), ("part", 4, 2), ("far", 4, 1),
+    ("part", 4, 3), ("end", 1), ("end", 2), ("last", 4),
 )
 
 
@@ -59,7 +61,7 @@
 class Plan:
     def __init__(self, wide, small):
         unit = wide // 2 // PARTS
-        self.half = [unit * size for size in SIZES]
+        self.half = [int(unit * size) for size in SIZES]
         self.width = [2 * half for half in self.half]
         self.first = [sum(self.half[:k]) for k in range(len(self.half))]
         self.row_wide = [int(width * share) for width, share in zip(self.width, ROW_FIRST)]
@@ -69,6 +71,15 @@
         self.row_total = max(8, sum(self.row_wide))
         self.dir_total = sum(self.width) - sum(self.row_wide)
         self.chunks = len(self.half)
+
+    def units_of(self, k):
+        return range(sum(UNITS[:k]), sum(UNITS[: k + 1]))
+
+    def unit_rows(self, u):
+        k = next(k for k in range(self.chunks) if u in self.units_of(k))
+        size = self.width[k] // UNITS[k]
+        start = 2 * self.first[k] + (u - sum(UNITS[:k])) * size
+        return slice(start, start + size)
 
     def rows(self, k):
         return slice(2 * self.first[k], 2 * self.first[k] + self.width[k])
@@ -164,17 +175,18 @@
             for part in range(2)
         ]
 
-    def send_dir(k, j):
-        rows = plan.rows(k)
-        return remote(sent.at[rows], dir_in.at[j - 1, rows], d_send.at[j - 1], d_recv.at[k, j - 1], dir_peer(j))
-
-    def send_x(k, j, which=None):
-        block_of = gathered.at[c if which is None else which, plan.rows(k)]
-        return remote(block_of, block_of, x_send.at[j - 1], x_recv.at[k, j - 1], x_peer(j))
-
-    def send_core(k, j, core_of):
-        block_of = gathered.at[from_x(j, core_of), plan.rows(k)]
-        return remote(block_of, block_of, c_send.at[0], c_recv.at[k, j], (d, r, partner))
+    def send_dir(u, j):
+        rows = plan.unit_rows(u)
+        return remote(sent.at[rows], dir_in.at[j - 1, rows], d_send.at[j - 1], d_recv.at[u, j - 1], dir_peer(j))
+
+    def send_x(u, j, which=None):
+        block_of = gathered.at[c if which is None else which, plan.unit_rows(u)]
+        return remote(block_of, block_of, x_send.at[j - 1], x_recv.at[u, j - 1], x_peer(j))
+
+    def send_core(u, j):
+        k = next(k for k in range(chunks) if u in plan.units_of(k))
+        block_of = gathered.at[from_x(j, core), plan.unit_rows(u)]
+        return remote(block_of, block_of, c_send.at[0], c_recv.at[k], (d, r, partner))
 
     def send_part(k, j, i):
         rows = plan.dir_rows(k)
@@ -188,7 +200,7 @@
 
     def send_row(k, i, p):
         rows = plan.dir_rows(k)
-        return remote(parts.at[0, i, rows], row_dir.at[p, rows], r_send.at[0], r_recv.at[k, p], row_peer(i))
+        return remote(parts.at[0, i, rows], row_dir.at[p, rows], r_send.at[0], r_recv.at[k], row_peer(i))
 
     def send_pair(k, i, j):
         return remote(
@@ -204,7 +216,7 @@
             parts.at[j, i, plan.row_rows(k)],
             row_in.at[r // 2, j, plan.row_slots(k)],
             q_send.at[0],
-            q_recv.at[k, r // 2],
+            q_recv.at[k],
             row_peer(i),
         )
 
@@ -272,29 +284,29 @@
 
         lax.fori_loop(0, n_far, body, 0)
 
-    def add_dirs(k):
-        rows = plan.rows(k)
+    def add_dirs(u):
+        rows = plan.unit_rows(u)
         for j in range(1, n_dir):
-            send_dir(k, j).wait_recv()
+            send_dir(u, j).wait_recv()
         total = sent[rows]
         for j in range(1, n_dir):
             total = total + dir_in[j - 1, rows]
         gathered[c, rows] = total
         for j in range(1, n_x):
-            send_x(k, j).start()
-        send_core(k, 0, core).start()
-
-    def relay(k):
+            send_x(u, j).start()
+        send_core(u, 0).start()
+
+    def relay(u):
         for j in range(1, n_x):
-            send_x(k, j, from_x(j, core)).wait_recv()
-            send_core(k, j, core).start()
+            send_x(u, j, from_x(j, core)).wait_recv()
+            send_core(u, j).start()
 
     per_far = n_near // n_far
 
     def make_sides(k):
         width, rows = plan.width[k], plan.rows(k)
-        for j in range(n_x):
-            send_core(k, j, CORES - 1 - core).wait_recv()
+        all_of = gathered.at[pl.ds(0, n_x), rows]
+        remote(all_of, all_of, c_send.at[0], c_recv.at[k], (d, r, partner)).wait_recv()
 
         def side(q, carry):
             values = gathered[q, rows]
@@ -392,10 +404,8 @@
 
     def add_rows(k):
         rows, slots = plan.row_rows(k), plan.row_slots(k)
-        for p in range(n_row // 2):
-            remote(
-                parts.at[:, own, rows], row_in.at[p, :, slots], q_send.at[0], q_recv.at[k, p], row_peer(n_cross)
-            ).wait_recv()
+        all_of = row_in.at[:, :, slots]
+        remote(all_of, all_of, q_send.at[0], q_recv.at[k], row_peer(n_cross)).wait_recv()
         for j in list(range(1, n_dir)) + [0]:
             total = parts[j, own, rows]
             for p in range(n_row // 2):
@@ -418,8 +428,9 @@
     def finish_dir(k):
         rows = plan.dir_rows(k)
         total = parts[0, own, rows]
+        all_of = row_dir.at[:, rows]
+        remote(all_of, all_of, r_send.at[0], r_recv.at[k], row_peer(n_cross)).wait_recv()
         for p in range(n_row // 2):
-            send_row(k, own, p).wait_recv()
             total = total + row_dir[p, rows]
         place(k, 0, total)
 
@@ -442,16 +453,16 @@
         for j in range(1, n_x):
             remote(gathered.at[0], gathered.at[0], x_send.at[j - 1], x_recv.at[0, 0], x_peer(1)).wait_send()
         all_of = gathered.at[pl.ds(0, n_x)]
-        remote(all_of, all_of, c_send.at[0], c_recv.at[0, 0], (d, r, partner)).wait_send()
+        remote(all_of, all_of, c_send.at[0], c_recv.at[0], (d, r, partner)).wait_send()
         dir_rows, row_rows = pl.ds(0, plan.dir_total), pl.ds(0, sum(plan.row_wide))
         if plan.dir_total > 0:
             all_of = parts.at[pl.ds(1, n_dir - 1), :, dir_rows]
             remote(all_of, all_of, p_send.at[0], p_recv.at[0, 0, 0], dir_peer(1)).wait_send()
             all_of = parts.at[0, pl.ds(0, own), dir_rows]
-            remote(all_of, all_of, r_send.at[0], r_recv.at[0, 0], row_peer(n_cross)).wait_send()
+            remote(all_of, all_of, r_send.at[0], r_recv.at[0], row_peer(n_cross)).wait_send()
         if sum(plan.row_wide) > 0:
             all_of = parts.at[:, pl.ds(0, own), row_rows]
-            remote(all_of, all_of, q_send.at[0], q_recv.at[0, 0], row_peer(n_cross)).wait_send()
+            remote(all_of, all_of, q_send.at[0], q_recv.at[0], row_peer(n_cross)).wait_send()
             all_of = parts.at[pl.ds(1, n_dir - 1), own, row_rows]
             remote(all_of, all_of, l_send.at[0], l_recv.at[0, 0], dir_peer(1)).wait_send()
 
@@ -470,8 +481,9 @@
         if group[0] == 0:
             pl.semaphore_wait(barrier, len(peers))
         for k in range(group[0], group[1] + 1):
-            for j in range(1, n_dir):
-                send_dir(k, j).start()
+            for u in plan.units_of(k):
+                for j in range(1, n_dir):
+                    send_dir(u, j).start()
 
     waiting = {k: (plan.row_wide[k] > 0) + (plan.row_wide[k] < plan.width[k]) for k in range(chunks)}
     put_at = [0]
@@ -556,19 +568,19 @@
             dma((stages,)),
             dma((2, 4)),
             dma((n_dir - 1,)),
-            dma((chunks, n_dir - 1)),
+            dma((sum(UNITS), n_dir - 1)),
             dma((n_x - 1,)),
-            dma((chunks, n_x - 1)),
+            dma((sum(UNITS), n_x - 1)),
             dma((1,)),
-            dma((chunks, n_x)),
+            dma((chunks,)),
             dma((1,)),
             dma((chunks, n_dir - 1, n_row)),
             dma((1,)),
             dma((chunks, n_row - 2)),
-            dma((chunks, n_row // 2)),
+            dma((chunks,)),
             dma((1,)),
             dma((chunks, n_row - 2)),
-            dma((chunks, n_row // 2)),
+            dma((chunks,)),
             dma((1,)),
             dma((chunks, n_dir - 1)),
         ],

time: 71.9 us -> 69.8 us (0.971)
  Pallas kernels: 70.9 us -> 68.8 us
    pallas_call x1, Pallas kernels: 70.9 us -> 68.8 us  [shards(): pl.pallas_call(functools.partial(kernel, n_dir, n_row, n_col, plan), out_...]
where the time goes in v4:
time: 69.8 us; the launch traced here: 69.6 us
  Pallas kernels  68.8 us (99%)
  local copies, waits for them, and re-layouts  0.8 us (1%)
    pallas_call x1, Pallas kernels, shards(): pl.pallas_call(functools.partial(kernel, n_dir, n_row, n_col, plan), out_...  68.8 us

profile of v4, /device:TPU:0, one launch (start us, length us, event | category | flops | bytes accessed | tf_op | source)
XLA Modules:
  0.0 69.6 jit_solution(10853433572351901128)
XLA Ops:
  0.0 68.8 %shard_map.91 = f32[256,512]{1,0:T(8,128)S(1)} custom-call(s32[2,8]{1,0:T(2,128)} %bitcast.2, s32[2,4]{1,0:T(2,128)} %bitcast.3, s32[4]{0:T(128)} %far_ranks.1, s32[1,2]{1,0:T(1,128)} %counts.1, bf16[1024,512]{1,0:T(8,128)(2,1)} %cot_hbm.1, bf16[2,512,1024]{2,1,0:T(8,128)(2,1)} %rad_hbm.1, f32[2,8,512,512]{3,2,1,0:T(8,128)} %near_z.1, ...), custom_call_target="tpu_custom_call" | custom-call | tf_op jit(solution)/shard_map/pallas_call | solution.py:539
  68.8 0.8 %copy.11 = f32[256,512]{1,0:T(8,128)} copy(f32[256,512]{1,0:T(8,128)S(1)} %shard_map.91) | data formatting | bytes 1048576
